TPU v7x, 32 devices: a whole 2x2x4 slice. The times are simulated.
32 devices in a mesh: dp: 8 (over y, x, core), seq: 4 (over z).
Axes of the slice: x: 2, y: 2, z: 4, core: 2. Of those that a mesh axis runs over, the one named last changes fastest.
Arguments:
- hidden_in: bfloat16 [8, 2048, 1024], P('dp', 'seq'), may hold values from -6 to 6
- doc_lengths: int32 [8, 8], P('dp'), may hold values from 1 to 1024, 2048 in all within a row
- ln1_gain: float32 [1024], replicated, may hold values from 0.1 to 1.9
- ln1_bias: float32 [1024], replicated, may hold values from -1.75 to 1.75
- ln2_gain: float32 [1024], replicated, may hold values from 0.1 to 1.9
- ln2_bias: float32 [1024], replicated, may hold values from -1.75 to 1.75
- qkv_weight: bfloat16 [1024, 3072], replicated, may hold values from -0.1875 to 0.1875
- qkv_bias: float32 [3072], replicated, may hold values from -1.75 to 1.75
- dense_weight: bfloat16 [1024, 1024], replicated, may hold values from -0.75 to 0.75
- dense_bias: float32 [1024], replicated, may hold values from -1.75 to 1.75
- fc_in_weight: bfloat16 [1024, 4096], replicated, may hold values from -0.1875 to 0.1875
- fc_in_bias: float32 [4096], replicated, may hold values from -1.75 to 1.75
- fc_out_weight: bfloat16 [4096, 1024], replicated, may hold values from -0.09375 to 0.09375
- fc_out_bias: float32 [1024], replicated, may hold values from -1.75 to 1.75
- out_grad: bfloat16 [8, 2048, 1024], P('dp', 'seq'), may hold values from -8 to 8
Outputs:
- hidden_out: bfloat16 [8, 2048, 1024], P('dp', 'seq')
- grad_in: float32 [8, 2048, 1024], P('dp', 'seq')
- grad_ln1_gain: float32 [1024], P(('dp', 'seq'))
- grad_ln1_bias: float32 [1024], P(('dp', 'seq'))
- grad_ln2_gain: float32 [1024], P(('dp', 'seq'))
- grad_ln2_bias: float32 [1024], P(('dp', 'seq'))
- grad_qkv_weight: float32 [1024, 3072], P(('dp', 'seq'))
- grad_qkv_bias: float32 [3072], P(('dp', 'seq'))
- grad_dense_weight: float32 [1024, 1024], P(('dp', 'seq'))
- grad_dense_bias: float32 [1024], P(('dp', 'seq'))
- grad_fc_in_weight: float32 [1024, 4096], P(('dp', 'seq'))
- grad_fc_in_bias: float32 [4096], P(('dp', 'seq'))
- grad_fc_out_weight: float32 [4096, 1024], P(('dp', 'seq'))
- grad_fc_out_bias: float32 [1024], P(('dp', 'seq'))
Inputs may be any that keep to these rules, and one draw needn't show every extreme that they name: `doc_lengths`: each row sums to 2048; its last entry is the padding document.
All inputs are finite; a program needn't handle non-finite values.
Results may differ from a plain program's by a relative error of at most 0.0097.
Values may be sent and summed in bfloat16 or wider, within the bound.
A program may use at most 256 MiB of HBM per device.

v0:
```python
import jax
import jax.numpy as jnp
from jax import lax
from jax.sharding import PartitionSpec as P

HEADS = 16
HEAD = 64
ROT = 16
epsilon = 1e-05
masked_score = -1e30


def layout(lengths, positions):
    doc_ends = jnp.cumsum(lengths, axis=1)
    starts = doc_ends - lengths
    segment = jnp.sum((positions[None, :, None] >= doc_ends[:, None, :]).astype(jnp.int32), axis=2)
    belongs = segment[:, :, None] == jnp.arange(lengths.shape[1], dtype=jnp.int32)[None, None, :]
    doc_start = jnp.sum(jnp.where(belongs, starts[:, None, :], 0), axis=2)
    return (segment, positions[None, :] - doc_start)


def standardize(values):
    average = jnp.mean(values, axis=-1, keepdims=True)
    centered = values - average
    variance = jnp.mean(centered * centered, axis=-1, keepdims=True)
    inv_std = lax.rsqrt(variance + epsilon)
    return (centered * inv_std, inv_std)


def norm_back(d_normed, unit, inv_std, gain):
    gain_grad = jnp.sum(d_normed * unit, axis=0)
    bias_grad = jnp.sum(d_normed, axis=0)
    d_unit = d_normed * gain
    d_input = inv_std * (
        d_unit
        - jnp.mean(d_unit, axis=-1, keepdims=True)
        - unit * jnp.mean(d_unit * unit, axis=-1, keepdims=True)
    )
    return (d_input, gain_grad, bias_grad)


def rotary_tables(positions):
    half_rot = ROT // 2
    inverse = 10000.0 ** (-(2.0 * jnp.arange(half_rot, dtype=jnp.float32)) / ROT)
    angle = positions.astype(jnp.float32)[:, None] * inverse[None, :]
    return (jnp.cos(angle)[:, None, None, :], jnp.sin(angle)[:, None, None, :])


def rotate(packed, cosine, sine_part):
    half_rot = cosine.shape[-1]
    first_half = packed[..., :half_rot]
    second_half = packed[..., half_rot : 2 * half_rot]
    turned = jnp.concatenate(
        [
            first_half * cosine - second_half * sine_part,
            second_half * cosine + first_half * sine_part,
            packed[..., 2 * half_rot :],
        ],
        axis=-1,
    )
    return jnp.concatenate([turned[..., :2, :], packed[..., 2:, :]], axis=-2)


def exact_gelu(values):
    return jax.nn.gelu(values, approximate=False)


def transpose_dot(left, right):
    return lax.dot_general(
        left, right, (((0,), (0,)), ((), ())), preferred_element_type=jnp.float32
    )


def masked_scores(queries, keys_all, seg_full, first_row, last_row, score_scale):
    scores = (
        jnp.einsum(
            "bqhd,bkhd->bhqk",
            queries[:, first_row:last_row],
            keys_all[:, :last_row],
            preferred_element_type=jnp.float32,
        )
        * score_scale
    )
    query_index = jnp.arange(first_row, last_row, dtype=jnp.int32)
    key_index = jnp.arange(last_row, dtype=jnp.int32)
    allowed = (seg_full[:, first_row:last_row, None] == seg_full[:, None, :last_row]) & (
        query_index[None, :, None] >= key_index[None, None, :]
    )
    return jnp.where(allowed[:, None], scores, masked_score)


def shards(
    hidden_in,
    doc_lengths,
    ln1_gain,
    ln1_bias,
    ln2_gain,
    ln2_bias,
    qkv_weight,
    qkv_bias,
    dense_weight,
    dense_bias,
    fc_in_weight,
    fc_in_bias,
    fc_out_weight,
    fc_out_bias,
    out_grad,
):
    seqs_here, local_len, model_width = hidden_in.shape
    seq_parts = lax.axis_size("seq")
    full_len = local_len * seq_parts
    heads_here = HEADS // seq_parts
    row_count = seqs_here * local_len
    score_scale = HEAD ** (-0.5)
    block_rows = min(512, full_len)
    local_pos = lax.axis_index("seq") * local_len + jnp.arange(local_len, dtype=jnp.int32)
    seg_local, pos_local = layout(doc_lengths, local_pos)
    live_rows = (seg_local < doc_lengths.shape[1] - 1).astype(jnp.float32).reshape(row_count, 1)
    input_f32 = hidden_in.astype(jnp.float32).reshape(row_count, model_width)
    unit_attn, inv_attn = standardize(input_f32)
    unit_mlp, inv_mlp = standardize(input_f32)
    normed_attn = (unit_attn * ln1_gain + ln1_bias).astype(jnp.bfloat16)
    normed_mlp = (unit_mlp * ln2_gain + ln2_bias).astype(jnp.bfloat16)
    qkv_f32 = jnp.dot(normed_attn, qkv_weight, preferred_element_type=jnp.float32) + qkv_bias
    shaped = qkv_f32.reshape(row_count, HEADS, 3, HEAD)
    cosine, sine_part = rotary_tables(pos_local.reshape(row_count))
    turned = (
        rotate(shaped, cosine, sine_part)
        .astype(jnp.bfloat16)
        .reshape(seqs_here, local_len, 3 * model_width)
    )
    head_side = lax.all_to_all(turned, "seq", split_axis=2, concat_axis=1, tiled=True).reshape(
        seqs_here, full_len, heads_here, 3, HEAD
    )
    queries = head_side[:, :, :, 0]
    keys_all = head_side[:, :, :, 1]
    values_all = head_side[:, :, :, 2]
    seg_full, _ = layout(doc_lengths, jnp.arange(full_len, dtype=jnp.int32))
    context_parts = []
    lse_parts = []
    for first_row in range(0, full_len, block_rows):
        last_row = first_row + block_rows
        scores = masked_scores(queries, keys_all, seg_full, first_row, last_row, score_scale)
        peak_score = jnp.max(scores, axis=-1, keepdims=True)
        exponentials = jnp.exp(scores - peak_score)
        weight_sum = jnp.sum(exponentials, axis=-1, keepdims=True)
        probability = exponentials / weight_sum
        lse_parts.append(peak_score[..., 0] + jnp.log(weight_sum[..., 0]))
        context_parts.append(
            jnp.einsum(
                "bhqk,bkhd->bqhd",
                probability.astype(jnp.bfloat16),
                values_all[:, :last_row],
                preferred_element_type=jnp.float32,
            )
        )
    context_heads = (
        jnp.concatenate(context_parts, axis=1)
        .astype(jnp.bfloat16)
        .reshape(seqs_here, full_len, heads_here * HEAD)
    )
    log_sums = jnp.concatenate(lse_parts, axis=2)
    context_tok = lax.all_to_all(
        context_heads, "seq", split_axis=1, concat_axis=2, tiled=True
    ).reshape(row_count, model_width)
    attn_branch = (
        jnp.dot(context_tok, dense_weight, preferred_element_type=jnp.float32) + dense_bias
    )
    pre_act = jnp.dot(normed_mlp, fc_in_weight, preferred_element_type=jnp.float32) + fc_in_bias
    activated, gelu_pull = jax.vjp(exact_gelu, pre_act)
    act_low = activated.astype(jnp.bfloat16)
    mlp_branch = jnp.dot(act_low, fc_out_weight, preferred_element_type=jnp.float32) + fc_out_bias
    hidden_out = (
        (input_f32 + attn_branch + mlp_branch)
        .astype(jnp.bfloat16)
        .reshape(seqs_here, local_len, model_width)
    )
    gradient = out_grad.astype(jnp.float32).reshape(row_count, model_width) * live_rows
    grad_low = gradient.astype(jnp.bfloat16)
    g_dense_w = transpose_dot(context_tok, grad_low)
    g_dense_b = jnp.sum(gradient, axis=0)
    d_context = jnp.dot(grad_low, dense_weight.T, preferred_element_type=jnp.float32).astype(
        jnp.bfloat16
    )
    d_context_heads = lax.all_to_all(
        d_context.reshape(seqs_here, local_len, model_width),
        "seq",
        split_axis=2,
        concat_axis=1,
        tiled=True,
    ).reshape(seqs_here, full_len, heads_here, HEAD)
    g_out_w = transpose_dot(act_low, grad_low)
    g_out_b = jnp.sum(gradient, axis=0)
    d_act = jnp.dot(grad_low, fc_out_weight.T, preferred_element_type=jnp.float32)
    d_pre = gelu_pull(d_act)[0].astype(jnp.bfloat16)
    g_in_w = transpose_dot(normed_mlp, d_pre)
    g_in_b = jnp.sum(d_pre.astype(jnp.float32), axis=0)
    d_mlp_in = jnp.dot(d_pre, fc_in_weight.T, preferred_element_type=jnp.float32)
    d_keys = jnp.zeros((seqs_here, full_len, heads_here, HEAD), jnp.float32)
    d_values = jnp.zeros((seqs_here, full_len, heads_here, HEAD), jnp.float32)
    d_query_parts = []
    for first_row in range(0, full_len, block_rows):
        last_row = first_row + block_rows
        scores = masked_scores(queries, keys_all, seg_full, first_row, last_row, score_scale)
        probability = jnp.exp(scores - log_sums[:, :, first_row:last_row, None])
        grad_rows = d_context_heads[:, first_row:last_row]
        d_values = d_values.at[:, :last_row].add(
            jnp.einsum(
                "bhqk,bqhd->bkhd",
                probability.astype(jnp.bfloat16),
                grad_rows,
                preferred_element_type=jnp.float32,
            )
        )
        d_prob = jnp.einsum(
            "bqhd,bkhd->bhqk",
            grad_rows,
            values_all[:, :last_row],
            preferred_element_type=jnp.float32,
        )
        row_delta = jnp.sum(probability * d_prob, axis=-1, keepdims=True)
        d_scores = (probability * (d_prob - row_delta)).astype(jnp.bfloat16)
        d_query_parts.append(
            jnp.einsum(
                "bhqk,bkhd->bqhd",
                d_scores,
                keys_all[:, :last_row],
                preferred_element_type=jnp.float32,
            )
            * score_scale
        )
        d_keys = d_keys.at[:, :last_row].add(
            jnp.einsum(
                "bhqk,bqhd->bkhd",
                d_scores,
                queries[:, first_row:last_row],
                preferred_element_type=jnp.float32,
            )
            * score_scale
        )
    d_queries = jnp.concatenate(d_query_parts, axis=1)
    d_heads = (
        jnp.stack([d_queries, d_keys, d_values], axis=3)
        .astype(jnp.bfloat16)
        .reshape(seqs_here, full_len, heads_here * 3 * HEAD)
    )
    d_tokens = lax.all_to_all(d_heads, "seq", split_axis=1, concat_axis=2, tiled=True).reshape(
        row_count, HEADS, 3, HEAD
    )
    _, rotate_pull = jax.vjp(lambda packed: rotate(packed, cosine, sine_part), shaped)
    d_qkv = (
        rotate_pull(d_tokens.astype(jnp.float32))[0]
        .reshape(row_count, 3 * model_width)
        .astype(jnp.bfloat16)
    )
    g_qkv_w = transpose_dot(normed_attn, d_qkv)
    g_qkv_b = jnp.sum(d_qkv.astype(jnp.float32), axis=0)
    d_attn_in = jnp.dot(d_qkv, qkv_weight.T, preferred_element_type=jnp.float32)
    dx_attn, g_gain_one, g_bias_one = norm_back(d_attn_in, unit_attn, inv_attn, ln1_gain)
    dx_mlp, g_gain_two, g_bias_two = norm_back(d_mlp_in, unit_mlp, inv_mlp, ln2_gain)
    grad_in = (gradient + dx_attn + dx_mlp).reshape(seqs_here, local_len, model_width)
    grad_terms = (
        g_gain_one,
        g_bias_one,
        g_gain_two,
        g_bias_two,
        g_qkv_w,
        g_qkv_b,
        g_dense_w,
        g_dense_b,
        g_in_w,
        g_in_b,
        g_out_w,
        g_out_b,
    )
    reduced = (
        lax.psum_scatter(grad_terms[0], ("dp", "seq"), scatter_dimension=0, tiled=True),
        lax.psum_scatter(grad_terms[1], ("dp", "seq"), scatter_dimension=0, tiled=True),
        lax.psum_scatter(grad_terms[2], ("dp", "seq"), scatter_dimension=0, tiled=True),
        lax.psum_scatter(grad_terms[3], ("dp", "seq"), scatter_dimension=0, tiled=True),
        lax.psum_scatter(grad_terms[4], ("dp", "seq"), scatter_dimension=0, tiled=True),
        lax.psum_scatter(grad_terms[5], ("dp", "seq"), scatter_dimension=0, tiled=True),
        lax.psum_scatter(grad_terms[6], ("dp", "seq"), scatter_dimension=0, tiled=True),
        lax.psum_scatter(grad_terms[7], ("dp", "seq"), scatter_dimension=0, tiled=True),
        lax.psum_scatter(grad_terms[8], ("dp", "seq"), scatter_dimension=0, tiled=True),
        lax.psum_scatter(grad_terms[9], ("dp", "seq"), scatter_dimension=0, tiled=True),
        lax.psum_scatter(grad_terms[10], ("dp", "seq"), scatter_dimension=0, tiled=True),
        lax.psum_scatter(grad_terms[11], ("dp", "seq"), scatter_dimension=0, tiled=True),
    )
    return (hidden_out, grad_in) + tuple(reduced)


def solution(mesh):
    return jax.shard_map(
        shards,
        mesh=mesh,
        in_specs=(
            P("dp", "seq", None),
            P("dp", None),
            P(),
            P(),
            P(),
            P(),
            P(),
            P(),
            P(),
            P(),
            P(),
            P(),
            P(),
            P(),
            P("dp", "seq", None),
        ),
        out_specs=(
            P("dp", "seq", None),
            P("dp", "seq", None),
            P(("dp", "seq")),
            P(("dp", "seq")),
            P(("dp", "seq")),
            P(("dp", "seq")),
            P(("dp", "seq"), None),
            P(("dp", "seq")),
            P(("dp", "seq"), None),
            P(("dp", "seq")),
            P(("dp", "seq"), None),
            P(("dp", "seq")),
            P(("dp", "seq"), None),
            P(("dp", "seq")),
        ),
        check_vma=False,
    )
```

profile of v0, /device:TPU:0, one launch (start us, length us, event | category | flops | bytes accessed | tf_op | source)
XLA Modules:
  0.0 1516.5 jit_solution(5117657675731257331)
XLA Ops:
  18.9 9.0 reduce.49
  31.7 6.9 all-to-all-start.2
  40.0 8.3 convolution_add_fusion
  48.3 6.6 copy.107
  61.1 27.4 %copy.139 = bf16[1,512,3072]{1,0,2:T(2,128)(2,1)} copy(bf16[1,512,3072]{1,2,0:T(8,128)(2,1)S(1)} %bitcast.395) | data formatting | bytes 6291456 | tf_op jit(solution)/shard_map/convert_element_type | solution.py:129
  88.6 22.0 %reduce.47 = bf16[3072,512]{1,0:T(8,128)(2,1)} reduce(bf16[3072,1,512]{2,1,0:T(2,128)(2,1)} %bitcast.392, bf16[]{:T(256)} %broadcast.808), dimensions={1}, to_apply=%bitcast.380.reduce_sub_computation | reduce | bytes 6291458
  136.2 55.2 %all-to-all-done = bf16[4,2,196608]{2,1,0:T(2,128)(2,1)} async-done(((bf16[4,2,196608]{2,1,0:T(2,128)(2,1)}), bf16[4,2,196608]{2,1,0:T(2,128)(2,1)}, u32[]{:S(2)}, u32[]{:S(2)}) %all-to-all-start) | async-done | bytes 3145760 | tf_op jit(solution)/shard_map/all_to_all | solution.py:132
  239.6 8.3 fusion.177
  248.0 8.1 fusion
  256.1 8.5 fusion.130
  294.6 7.6 multiply_convert_fusion.1
  315.2 12.7 fusion.181
  328.0 12.6 reduce.48
  348.4 11.5 multiply_reduce_fusion
  359.9 11.9 multiply_convert_fusion
  403.1 8.6 fusion.71
  414.2 15.7 %copy.125 = bf16[1,2048,768]{2,0,1:T(2,128)(2,1)} copy(bf16[1,2048,768]{1,2,0:T(8,128)(2,1)} %bitcast.397) | data formatting | bytes 6291456 | tf_op jit(solution)/shard_map/convert_element_type | solution.py:244
  429.9 33.3 %reduce.50 = bf16[2048,768]{1,0:T(8,128)(2,1)} reduce(bf16[2048,1,768]{2,1,0:T(2,128)(2,1)} %bitcast.391, bf16[]{:T(256)} %broadcast.808), dimensions={1}, to_apply=%bitcast.316.reduce_sub_computation | reduce | bytes 6291458
  467.7 118.8 %all_to_all.54 = bf16[4,2,196608]{2,1,0:T(2,128)(2,1)} all-to-all(bf16[4,2,196608]{2,1,0:T(2,128)(2,1)} %reshape.1434), channel_id=1, replica_groups=mesh['dp'=8,'seq'=4] {'seq'}, dimensions={0} | all-to-all | bytes 6291456 | tf_op jit(solution)/shard_map/all_to_all | solution.py:247
  599.2 6.5 copy.127
  614.6 6.9 fusion.136
  622.3 27.9 %multiply_convert_fusion.3 = (bf16[512,4096]{1,0:T(8,128)(2,1)}, f32[512,4096]{1,0:T(8,128)}, f32[512,4096]{1,0:T(8,128)}) fusion(f32[4096]{0:T(1024)S(1)} %copy-done.45, bf16[1024,4096]{1,0:T(8,128)(2,1)} %param.45, bf16[1,512,1024]{2,1,0:T(8,128)(2,1)S(1)} %copy-done.13, f32[1024]{0:T(1024)S(1)} %copy-done.49, f32[1024]{0:T(1024)S(1)} %copy-done.41, ...), kind=kOutput, calls=%fused_computation.25 | convolution fusion | flops 4436525056 | bytes 30437376 | tf_op jit(solution)/shard_map/dot_general | solution.py:169
  650.2 14.5 convert_reduce_fusion
  666.7 8.4 fusion.171
  675.4 13.4 fusion.164
  688.8 10.7 fusion.183
  699.5 7.3 fusion.182
  709.3 9.4 fusion.87
  721.4 41.4 %all-reduce.13 = (f32[1024]{0:T(1024)S(1)}, f32[1024]{0:T(1024)S(1)}, f32[1024]{0:T(1024)S(1)}, f32[1024]{0:T(1024)S(1)}, f32[3072]{0:T(1024)S(1)}, /*index=5*/f32[1024]{0:T(1024)S(1)}, f32[4096]{0:T(1024)S(1)}) all-reduce(f32[1024]{0:T(1024)S(1)} %get-tuple-element.128, ...), channel_id=2, replica_groups=mesh['dp'=8,'seq'=4] {'dp','seq'}, use_global_device_ids=true, to_apply=%region_23.24.clone | all-reduce | flops 12288 | bytes 98304
  766.3 11.3 reduce-scatter.5.cloned.1.call-done
  777.7 366.3 %reduce-scatter.9.cloned.1.call-done = f32[32,4096]{1,0:T(8,128)} async-done(((f32[1024,4096]{1,0:T(8,128)}), f32[32,4096]{1,0:T(8,128)}) %reduce-scatter.9.cloned.1.call-update) | async-done | bytes 524304 | tf_op jit(solution)/shard_map/reduce_scatter | solution.py:285
  1143.9 365.0 %reduce-scatter.11.cloned.1.call-done = f32[128,1024]{1,0:T(8,128)} async-done(((f32[4096,1024]{1,0:T(8,128)}), f32[128,1024]{1,0:T(8,128)}) %reduce-scatter.11.cloned.1.call-update) | async-done | bytes 524304 | tf_op jit(solution)/shard_map/reduce_scatter | solution.py:287
  (250 shorter events, 219.1 us)
Async XLA Ops:
  12.4 26.2 %copy-start.12 = (bf16[1,512,1024]{2,1,0:T(8,128)(2,1)S(1)}, bf16[1,512,1024]{2,1,0:T(8,128)(2,1)}, u32[]{:S(2)}) copy-start(bf16[1,512,1024]{2,1,0:T(8,128)(2,1)} %param.35) | copy-start | bytes 3145732
  18.9 21.1 %copy-start.42 = (f32[1024]{0:T(1024)S(1)}, f32[1024]{0:T(1024)}, u32[]{:S(2)}) copy-start(f32[1024]{0:T(1024)} %param.37) | copy-start | bytes 12292
  18.9 21.1 %copy-start.46 = (f32[3072]{0:T(1024)S(1)}, f32[3072]{0:T(1024)}, u32[]{:S(2)}) copy-start(f32[3072]{0:T(1024)} %param.42) | copy-start | bytes 36868
  18.9 21.1 %copy-start.47 = (f32[1024]{0:T(1024)S(1)}, f32[1024]{0:T(1024)}, u32[]{:S(2)}) copy-start(f32[1024]{0:T(1024)} %param.38) | copy-start | bytes 12292
  31.7 84.1 %all-to-all-start.2 = ((bf16[4,2,65536]{2,1,0:T(2,128)(2,1)}), bf16[4,2,65536]{2,1,0:T(2,128)(2,1)}, u32[]{:S(2)}, u32[]{:S(2)}) async-start(bf16[4,2,65536]{2,1,0:T(2,128)(2,1)} %reshape.1432), calls=%async_computation.2 | async-start | bytes 2097152 | tf_op jit(solution)/shard_map/all_to_all | solution.py:185
  115.8 75.6 %all-to-all-start = ((bf16[4,2,196608]{2,1,0:T(2,128)(2,1)}), bf16[4,2,196608]{2,1,0:T(2,128)(2,1)}, u32[]{:S(2)}, u32[]{:S(2)}) async-start(bf16[4,2,196608]{2,1,0:T(2,128)(2,1)} %reshape.1428), calls=%async_computation | async-start | bytes 6291456 | tf_op jit(solution)/shard_map/all_to_all | solution.py:132
  213.9 11.3 copy-start.14
  213.9 13.4 copy-start.16
  213.9 13.4 copy-start.19
  266.5 10.7 slice-start.3
  266.5 7.5 copy-start.23
  266.5 10.7 slice-start.4
  271.3 10.2 copy-start.10
  294.6 9.7 slice-start.5
  294.6 7.6 copy-start.17
  294.6 9.6 slice-start.6
  344.1 44.0 %all-to-all-start.1 = ((bf16[4,2,65536]{2,1,0:T(2,128)(2,1)}), bf16[4,2,65536]{2,1,0:T(2,128)(2,1)}, u32[]{:S(2)}, u32[]{:S(2)}) async-start(bf16[4,2,65536]{2,1,0:T(2,128)(2,1)} %reshape.1430), calls=%async_computation.1 | async-start | bytes 2097152 | tf_op jit(solution)/shard_map/all_to_all | solution.py:163
  348.3 418.0 %reduce-scatter.7.cloned.1.call-start = ((), (), s32[]{:S(2)}) async-start(), calls=%async_computation.9 | async-start | bytes 4325376 | tf_op jit(solution)/shard_map/reduce_scatter | solution.py:283
  359.9 16.7 %copy-start.18 = (bf16[1,2048,4,64]{1,3,2,0:T(8,128)(2,1)S(1)}, bf16[1,2048,4,64]{1,3,2,0:T(8,128)(2,1)}, u32[]{:S(2)}) copy-start(bf16[1,2048,4,64]{1,3,2,0:T(8,128)(2,1)} %copy-done.16) | copy-start | bytes 3145732
  371.8 11.8 slice-start
  388.0 9.0 copy-start.38
  401.9 375.8 %reduce-scatter.5.cloned.1.call-start = ((), (), s32[]{:S(2)}) async-start(), calls=%async_computation.8 | async-start | bytes 12976128 | tf_op jit(solution)/shard_map/reduce_scatter | solution.py:281
  403.1 8.6 copy-start.21
  599.2 8.3 copy-start.44
  621.6 522.4 %reduce-scatter.9.cloned.1.call-start = ((), (), s32[]{:S(2)}) async-start(), calls=%async_computation.10 | async-start | bytes 17301504 | tf_op jit(solution)/shard_map/reduce_scatter | solution.py:285
  622.3 27.9 %copy-start.27 = (bf16[1,512,1024]{2,1,0:T(8,128)(2,1)S(1)}, bf16[1,512,1024]{2,1,0:T(8,128)(2,1)}, u32[]{:S(2)}) copy-start(bf16[1,512,1024]{2,1,0:T(8,128)(2,1)} %param.49) | copy-start | bytes 3145732
  675.1 833.8 %reduce-scatter.11.cloned.1.call-start = ((), (), s32[]{:S(2)}) async-start(), calls=%async_computation.11 | async-start | bytes 17301504 | tf_op jit(solution)/shard_map/reduce_scatter | solution.py:287
  688.8 10.7 copy-start.54
  699.5 7.4 copy-start.51
  709.3 9.4 copy-start.24
  709.3 9.4 copy-start.28
  763.4 746.1 %copy-start.53 = (f32[32]{0:T(128)}, f32[32]{0:T(128)S(1)}, u32[]{:S(2)}) copy-start(f32[32]{0:T(128)S(1)} %dynamic-slice.67) | copy-start | bytes 388
  (38 other events, 113.4 us)
Sparse Core Ops, SparseCore 0:
  402.0 176.7 reduce-scatter.6
  621.7 155.9 reduce-scatter.4
  780.6 363.2 reduce-scatter.8
  1146.8 362.1 reduce-scatter.10
where the time goes:
time: 1530 us; the launch traced here: 1520 us
  waiting for transfers between devices  798 us (52%)
  matrix products  210 us (14%)
  local copies, waits for them, and re-layouts  160 us (10%)
  blocking collectives  160 us (10%)
  other arithmetic  156 us (10%)
  starting transfers between devices  16.8 us (1%)
    reduce_scatter x1, waiting for transfers between devices, shards(): lax.psum_scatter(grad_terms[8], ('dp', 'seq'), scatter_dimension=0, tiled...  366 us
    reduce_scatter x1, waiting for transfers between devices, shards(): lax.psum_scatter(grad_terms[10], ('dp', 'seq'), scatter_dimension=0, tile...  365 us
    all_to_all x1, blocking collectives, shards(): lax.all_to_all(d_heads, 'seq', split_axis=1, concat_axis=2, tiled=True)  119 us
    unnamed x8, other arithmetic  89.7 us
    unnamed x146, local copies, waits for them, and re-layouts  61.3 us
    all_to_all x1, waiting for transfers between devices, shards(): lax.all_to_all(turned, 'seq', split_axis=2, concat_axis=1, tiled=True)  55.2 us
    unnamed x1, blocking collectives  41.4 us
    dot_general x4, matrix products, transpose_dot(): lax.dot_general(left, right, (((0,), (0,)), ((), ())), preferred_element_...  33.6 us
  transfers between devices with their start and end apart: 7, of which 4 were waited for; matrix products, arithmetic and copies ran while one was open for 22% of the time, Pallas kernels for 0%

commit v1 on v0

--- a/solution.py
+++ b/solution.py
@@ -8,6 +8,22 @@
 ROT = 16
 epsilon = 1e-05
 masked_score = -1e30
+
+
+def pairwise_exchange(shard, axis, split, join):
+    ways, here = (lax.axis_size(axis), lax.axis_index(axis))
+    width = shard.shape[split] // ways
+    shape = list(shard.shape)
+    shape[split] = width
+    height = shape[join]
+    shape[join] = height * ways
+    full = jnp.zeros(shape, shard.dtype)
+    for mask in range(ways):
+        part = lax.dynamic_slice_in_dim(shard, (here ^ mask) * width, width, axis=split)
+        if mask:
+            part = lax.ppermute(part, axis, [(d, d ^ mask) for d in range(ways)])
+        full = lax.dynamic_update_slice_in_dim(full, part, (here ^ mask) * height, axis=join)
+    return full
 
 
 def layout(lengths, positions):
@@ -129,7 +145,7 @@
         .astype(jnp.bfloat16)
         .reshape(seqs_here, local_len, 3 * model_width)
     )
-    head_side = lax.all_to_all(turned, "seq", split_axis=2, concat_axis=1, tiled=True).reshape(
+    head_side = pairwise_exchange(turned, "seq", 2, 1).reshape(
         seqs_here, full_len, heads_here, 3, HEAD
     )
     queries = head_side[:, :, :, 0]

time: 1530 us -> 1470 us (0.961)
  local copies, waits for them, and re-layouts: 160 us -> 112 us
  other arithmetic: 156 us -> 134 us
  matrix products: 210 us -> 226 us
    ppermute x0 -> x3, waiting for transfers between devices: none -> 58.7 us  [pairwise_exchange(): part = lax.ppermute(part, axis, [(d, d ^ mask) for d in range(ways)])]
    all_to_all x1 -> x0, waiting for transfers between devices: 55.2 us -> none  [shards(): lax.all_to_all(turned, 'seq', split_axis=2, concat_axis=1, tiled=True)]
    convert_element_type x1 -> x0, local copies, waits for them, and re-layouts: 27.4 us -> none  [shards(): turned = rotate(shaped, cosine, sine_part).astype(jnp.bfloat16).reshape(s...]
    unnamed x8, other arithmetic: 89.7 us -> 69.9 us
    unnamed x146 -> x143, local copies, waits for them, and re-layouts: 61.3 us -> 44.5 us
  transfers between devices with their start and end apart: 7 -> 9, of which waited for: 4 -> 5; matrix products, arithmetic and copies ran while one was open for 22% -> 29% of each run, Pallas kernels for 0% -> 0%
where the time goes in v1:
time: 1470 us; the launch traced here: 1460 us
  waiting for transfers between devices  800 us (54%)
  matrix products  226 us (15%)
  blocking collectives  161 us (11%)
  other arithmetic  134 us (9%)
  local copies, waits for them, and re-layouts  112 us (8%)
  starting transfers between devices  15.8 us (1%)
  between operations  15 us (1%)
    reduce_scatter x1, waiting for transfers between devices, shards(): lax.psum_scatter(grad_terms[8], ('dp', 'seq'), scatter_dimension=0, tiled...  366 us
    reduce_scatter x1, waiting for transfers between devices, shards(): lax.psum_scatter(grad_terms[10], ('dp', 'seq'), scatter_dimension=0, tile...  365 us
    all_to_all x1, blocking collectives, shards(): lax.all_to_all(d_heads, 'seq', split_axis=1, concat_axis=2, tiled=True)  119 us
    unnamed x8, other arithmetic  69.9 us
    ppermute x3, waiting for transfers between devices, pairwise_exchange(): part = lax.ppermute(part, axis, [(d, d ^ mask) for d in range(ways)])  58.7 us
    unnamed x143, local copies, waits for them, and re-layouts  44.5 us
    unnamed x1, blocking collectives  41.9 us
    dot_general x4, matrix products, transpose_dot(): lax.dot_general(left, right, (((0,), (0,)), ((), ())), preferred_element_...  34.4 us
  transfers between devices with their start and end apart: 9, of which 5 were waited for; matrix products, arithmetic and copies ran while one was open for 29% of the time, Pallas kernels for 0%

profile of v1, /device:TPU:0, one launch (start us, length us, event | category | flops | bytes accessed | tf_op | source)
XLA Modules:
  0.0 1462.6 jit_solution(15148836732180316506)
XLA Ops:
  15.8 9.0 reduce.48
  28.6 6.8 all-to-all-start.1
  36.8 8.3 convolution_add_fusion
  45.1 6.6 copy.101
  74.1 43.9 %collective-permute-done = bf16[1,512,768]{1,2,0:T(8,128)(2,1)} collective-permute-done((bf16[1,512,768]{1,2,0:T(8,128)(2,1)}, bf16[1,512,768]{1,2,0:T(8,128)(2,1)}, u32[]{:S(2)}, u32[]{:S(2)}) %collective-permute-start) | collective-permute-done | bytes 786464 | tf_op jit(solution)/shard_map/ppermute | solution.py:24
  120.1 14.8 %collective-permute-done.1 = bf16[1,512,768]{1,2,0:T(8,128)(2,1)} collective-permute-done((bf16[1,512,768]{1,2,0:T(8,128)(2,1)}, bf16[1,512,768]{1,2,0:T(8,128)(2,1)}, u32[]{:S(2)}, u32[]{:S(2)}) %collective-permute-start.1) | collective-permute-done | bytes 786464 | tf_op jit(solution)/shard_map/ppermute | solution.py:24
  167.8 10.6 fusion.177
  178.4 8.1 fusion
  186.5 8.0 fusion.130
  195.6 15.9 %fusion.181 = bf16[2048,1,256]{2,1,0:T(2,128)(2,1)} fusion(bf16[1,512,256]{2,0,1:T(2,128)(2,1)} %copy.109, bf16[1,512,256]{2,0,1:T(2,128)(2,1)} %copy.108, bf16[1,512,256]{2,0,1:T(2,128)(2,1)S(1)} %copy-done.22, bf16[1,512,256]{2,0,1:T(2,128)(2,1)S(1)} %copy-done.21), kind=kLoop, calls=%fused_computation.263 | loop fusion | flops 1572864 | bytes 2097152
  211.5 11.6 reduce.47
  275.7 7.1 multiply_convert_fusion.2
  292.2 9.2 multiply_reduce_fusion
  301.5 10.2 multiply_convert_fusion
  311.7 7.2 fusion.133
  349.7 8.4 fusion.71
  360.6 15.8 %copy.117 = bf16[1,2048,768]{2,0,1:T(2,128)(2,1)} copy(bf16[1,2048,768]{1,2,0:T(8,128)(2,1)} %bitcast.388) | data formatting | bytes 6291456 | tf_op jit(solution)/shard_map/convert_element_type | solution.py:260
  376.4 33.3 %reduce.49 = bf16[2048,768]{1,0:T(8,128)(2,1)} reduce(bf16[2048,1,768]{2,1,0:T(2,128)(2,1)} %bitcast.385, bf16[]{:T(256)} %broadcast.808), dimensions={1}, to_apply=%bitcast.310.reduce_sub_computation | reduce | bytes 6291458
  414.3 118.9 %all_to_all.39 = bf16[4,2,196608]{2,1,0:T(2,128)(2,1)} all-to-all(bf16[4,2,196608]{2,1,0:T(2,128)(2,1)} %reshape.1431), channel_id=1, replica_groups=mesh['dp'=8,'seq'=4] {'seq'}, dimensions={0} | all-to-all | bytes 6291456 | tf_op jit(solution)/shard_map/all_to_all | solution.py:263
  545.9 6.5 copy.119
  561.4 6.9 fusion.136
  569.0 28.1 %multiply_convert_fusion.3 = (bf16[512,4096]{1,0:T(8,128)(2,1)}, f32[512,4096]{1,0:T(8,128)}, f32[512,4096]{1,0:T(8,128)}) fusion(f32[4096]{0:T(1024)S(1)} %copy-done.40, bf16[1024,4096]{1,0:T(8,128)(2,1)} %param.45, bf16[1,512,1024]{2,1,0:T(8,128)(2,1)S(1)} %copy-done.12, f32[1024]{0:T(1024)S(1)} %copy-done.44, f32[1024]{0:T(1024)S(1)} %copy-done.36, ...), kind=kOutput, calls=%fused_computation.25 | convolution fusion | flops 4436525056 | bytes 30437376 | tf_op jit(solution)/shard_map/dot_general | solution.py:185
  597.1 14.5 convert_reduce_fusion
  613.6 8.7 fusion.171
  622.6 14.0 fusion.164
  636.6 10.7 fusion.183
  647.4 7.4 fusion.182
  657.2 9.3 fusion.87
  669.1 41.9 %all-reduce.13 = (f32[1024]{0:T(1024)S(1)}, f32[1024]{0:T(1024)S(1)}, f32[1024]{0:T(1024)S(1)}, f32[1024]{0:T(1024)S(1)}, f32[3072]{0:T(1024)S(1)}, /*index=5*/f32[1024]{0:T(1024)S(1)}, f32[4096]{0:T(1024)S(1)}) all-reduce(f32[1024]{0:T(1024)S(1)} %get-tuple-element.128, ...), channel_id=2, replica_groups=mesh['dp'=8,'seq'=4] {'dp','seq'}, use_global_device_ids=true, to_apply=%region_23.24.clone | all-reduce | flops 12288 | bytes 98304
  714.6 9.4 reduce-scatter.5.cloned.1.call-done
  724.0 366.3 %reduce-scatter.9.cloned.1.call-done = f32[32,4096]{1,0:T(8,128)} async-done(((f32[1024,4096]{1,0:T(8,128)}), f32[32,4096]{1,0:T(8,128)}) %reduce-scatter.9.cloned.1.call-update) | async-done | bytes 524304 | tf_op jit(solution)/shard_map/reduce_scatter | solution.py:301
  1090.3 365.0 %reduce-scatter.11.cloned.1.call-done = f32[128,1024]{1,0:T(8,128)} async-done(((f32[4096,1024]{1,0:T(8,128)}), f32[128,1024]{1,0:T(8,128)}) %reduce-scatter.11.cloned.1.call-update) | async-done | bytes 524304 | tf_op jit(solution)/shard_map/reduce_scatter | solution.py:303
  (253 shorter events, 204.9 us)
Async XLA Ops:
  15.3 20.1 %copy-start.47 = (s32[1,8]{1,0:T(1,128)S(1)}, s32[1,8]{1,0:T(1,128)}, u32[]{:S(2)}) copy-start(s32[1,8]{1,0:T(1,128)} %param.36) | copy-start | bytes 100
  15.3 20.2 %copy-start.11 = (bf16[1,512,1024]{2,1,0:T(8,128)(2,1)S(1)}, bf16[1,512,1024]{2,1,0:T(8,128)(2,1)}, u32[]{:S(2)}) copy-start(bf16[1,512,1024]{2,1,0:T(8,128)(2,1)} %param.35) | copy-start | bytes 3145732
  15.8 21.0 %copy-start.37 = (f32[1024]{0:T(1024)S(1)}, f32[1024]{0:T(1024)}, u32[]{:S(2)}) copy-start(f32[1024]{0:T(1024)} %param.37) | copy-start | bytes 12292
  15.8 21.0 %copy-start.41 = (f32[3072]{0:T(1024)S(1)}, f32[3072]{0:T(1024)}, u32[]{:S(2)}) copy-start(f32[3072]{0:T(1024)} %param.42) | copy-start | bytes 36868
  15.8 21.0 %copy-start.42 = (f32[1024]{0:T(1024)S(1)}, f32[1024]{0:T(1024)}, u32[]{:S(2)}) copy-start(f32[1024]{0:T(1024)} %param.38) | copy-start | bytes 12292
  28.6 196.3 %all-to-all-start.1 = ((bf16[4,2,65536]{2,1,0:T(2,128)(2,1)}), bf16[4,2,65536]{2,1,0:T(2,128)(2,1)}, u32[]{:S(2)}, u32[]{:S(2)}) async-start(bf16[4,2,65536]{2,1,0:T(2,128)(2,1)} %reshape.1429), calls=%async_computation.1 | async-start | bytes 2097152 | tf_op jit(solution)/shard_map/all_to_all | solution.py:201
  64.0 73.0 %collective-permute-start.2 = (bf16[1,512,768]{1,2,0:T(8,128)(2,1)S(1)}, bf16[1,512,768]{1,2,0:T(8,128)(2,1)}, u32[]{:S(2)}, u32[]{:S(2)}) collective-permute-start(bf16[1,512,768]{1,2,0:T(8,128)(2,1)S(1)} %get-tuple-element.156), channel_id=1, source_target_pairs={{0,3},{1,2},{2,1},{3,0},{4,7},{5,6},{6,5},{7,4},{8,11},{9,10},{10,... | collective-permute-start | bytes 2359304 | tf_op jit(solution)/shard_map/ppermute | solution.py:24
  67.9 67.0 %collective-permute-start.1 = (bf16[1,512,768]{1,2,0:T(8,128)(2,1)}, bf16[1,512,768]{1,2,0:T(8,128)(2,1)}, u32[]{:S(2)}, u32[]{:S(2)}) collective-permute-start(bf16[1,512,768]{1,2,0:T(8,128)(2,1)} %get-tuple-element.157), channel_id=1, source_target_pairs={{0,2},{1,3},{2,0},{3,1},{4,6},{5,7},{6,4},{7,5},{8,10},{9,11},{10,... | collective-permute-start | bytes 2359304 | tf_op jit(solution)/shard_map/ppermute | solution.py:24
  67.9 50.1 %collective-permute-start = (bf16[1,512,768]{1,2,0:T(8,128)(2,1)}, bf16[1,512,768]{1,2,0:T(8,128)(2,1)}, u32[]{:S(2)}, u32[]{:S(2)}) collective-permute-start(bf16[1,512,768]{1,2,0:T(8,128)(2,1)} %get-tuple-element.158), channel_id=1, source_target_pairs={{0,1},{1,0},{2,3},{3,2},{4,5},{5,4},{6,7},{7,6},{8,9},{9,8},{10,11... | collective-permute-start | bytes 2359304 | tf_op jit(solution)/shard_map/ppermute | solution.py:24
  141.3 19.5 %copy-start.13 = (bf16[1,2048,4,64]{1,3,2,0:T(8,128)(2,1)}, bf16[1,2048,4,64]{1,3,2,0:T(8,128)(2,1)S(1)}, u32[]{:S(2)}) copy-start(bf16[1,2048,4,64]{1,3,2,0:T(8,128)(2,1)S(1)} %get-tuple-element.153) | copy-start | bytes 3145732
  186.5 9.1 copy-start.21
  186.5 9.1 copy-start.22
  224.9 109.7 %all-to-all-start = ((bf16[4,2,65536]{2,1,0:T(2,128)(2,1)}), bf16[4,2,65536]{2,1,0:T(2,128)(2,1)}, u32[]{:S(2)}, u32[]{:S(2)}) async-start(bf16[4,2,65536]{2,1,0:T(2,128)(2,1)} %reshape.1427), calls=%async_computation | async-start | bytes 2097152 | tf_op jit(solution)/shard_map/all_to_all | solution.py:179
  229.2 485.4 %reduce-scatter.7.cloned.1.call-start = ((), (), s32[]{:S(2)}) async-start(), calls=%async_computation.8 | async-start | bytes 4325376 | tf_op jit(solution)/shard_map/reduce_scatter | solution.py:299
  239.1 22.2 %copy-start.9 = (bf16[1,2048,4,64]{1,3,2,0:T(8,128)(2,1)}, bf16[1,2048,4,64]{1,3,2,0:T(8,128)(2,1)S(1)}, u32[]{:S(2)}) copy-start(bf16[1,2048,4,64]{1,3,2,0:T(8,128)(2,1)S(1)} %reshape.1415) | copy-start | bytes 3145732
  275.7 16.5 %slice-start = ((s8[16777216]{0:T(1024)(128)(4,1)}), s8[4194304]{0:T(1024)(128)(4,1)S(1)}, s32[]{:S(2)}) async-start(s8[16777216]{0:T(1024)(128)(4,1)} %bitcast.373), calls=%async_computation.11 | async-start | bytes 8388608
  275.7 16.5 %slice-start.1 = ((s8[16777216]{0:T(1024)(128)(4,1)}), s8[4194304]{0:T(1024)(128)(4,1)S(1)}, s32[]{:S(2)}) async-start(s8[16777216]{0:T(1024)(128)(4,1)} %bitcast.373), calls=%async_computation.12 | async-start | bytes 8388608
  275.7 16.5 %slice-start.2 = ((s8[16777216]{0:T(1024)(128)(4,1)}), s8[4194304]{0:T(1024)(128)(4,1)S(1)}, s32[]{:S(2)}) async-start(s8[16777216]{0:T(1024)(128)(4,1)} %bitcast.373), calls=%async_computation.13 | async-start | bytes 8388608
  282.8 9.4 slice-start.3
  311.7 14.7 %copy-start.3 = (bf16[4,512,2048]{2,1,0:T(8,128)(2,1)S(1)}, bf16[4,512,2048]{2,1,0:T(8,128)(2,1)}, u32[]{:S(2)}) copy-start(bf16[4,512,2048]{2,1,0:T(8,128)(2,1)} %multiply_convert_fusion) | copy-start | bytes 25165828
  311.7 14.7 %copy-start.7 = (f32[1,2048,4,64]{1,3,2,0:T(8,128)S(1)}, f32[1,2048,4,64]{1,3,2,0:T(8,128)}, u32[]{:S(2)}) copy-start(f32[1,2048,4,64]{1,3,2,0:T(8,128)} %fusion.36) | copy-start | bytes 6291460
  311.7 18.4 %slice-start.7 = ((s8[12582912]{0:T(1024)(128)(4,1)}), s8[4194304]{0:T(1024)(128)(4,1)S(1)}, s32[]{:S(2)}) async-start(s8[12582912]{0:T(1024)(128)(4,1)} %bitcast.377), calls=%async_computation.18 | async-start | bytes 8388608
  319.0 11.2 slice-start.8
  334.6 9.0 copy-start.33
  348.4 375.6 %reduce-scatter.5.cloned.1.call-start = ((), (), s32[]{:S(2)}) async-start(), calls=%async_computation.7 | async-start | bytes 12976128 | tf_op jit(solution)/shard_map/reduce_scatter | solution.py:297
  568.3 522.1 %reduce-scatter.9.cloned.1.call-start = ((), (), s32[]{:S(2)}) async-start(), calls=%async_computation.9 | async-start | bytes 17301504 | tf_op jit(solution)/shard_map/reduce_scatter | solution.py:301
  569.0 28.1 %copy-start.24 = (bf16[1,512,1024]{2,1,0:T(8,128)(2,1)S(1)}, bf16[1,512,1024]{2,1,0:T(8,128)(2,1)}, u32[]{:S(2)}) copy-start(bf16[1,512,1024]{2,1,0:T(8,128)(2,1)} %param.49) | copy-start | bytes 3145732
  622.4 833.0 %reduce-scatter.11.cloned.1.call-start = ((), (), s32[]{:S(2)}) async-start(), calls=%async_computation.10 | async-start | bytes 17301504 | tf_op jit(solution)/shard_map/reduce_scatter | solution.py:303
  636.6 10.8 copy-start.49
  657.2 9.3 copy-start.20
  657.2 9.3 copy-start.25
  711.7 744.2 %copy-start.48 = (f32[32]{0:T(128)}, f32[32]{0:T(128)S(1)}, u32[]{:S(2)}) copy-start(f32[32]{0:T(128)S(1)} %dynamic-slice.67) | copy-start | bytes 388
  (40 other events, 142.5 us)
Sparse Core Ops, SparseCore 0:
  348.5 176.7 reduce-scatter.6
  568.4 155.5 reduce-scatter.4
  727.0 363.3 reduce-scatter.8
  1093.2 362.1 reduce-scatter.10
